TPU v7x, 256 devices: a whole 4x4x8 slice. The times are simulated.
256 devices in a mesh: freq: 32 (over z, x), brow: 2 (over y_hi), bcol: 4 (over y_lo, core).
Axes of the slice: x: 4, y: 4 (y_hi: 2, y_lo: 2; y = y_hi * 2 + y_lo), z: 8, core: 2. Of those that a mesh axis runs over, the one named last changes fastest.
Arguments:
- voltages: bfloat16 [2, 1024, 94208], P(None, ('brow', 'bcol', 'freq')), may hold values from -6 to 6
- fir_taps: float32 [16, 4096], replicated, may hold values from -1.5 to 1.5
Outputs:
- visibilities: float32 [2, 128, 1024, 2, 4, 128], P(None, 'freq', 'brow', None, 'bcol')
All inputs are finite; a program needn't handle non-finite values.
Results may differ from a plain program's by a relative error of at most 0.0036.
Values may be sent and summed in bfloat16 or wider, within the bound.
A program may use at most 64 MiB of HBM per device.

v0:
```python
import math
import jax
import jax.numpy as jnp
from jax import lax
from jax.sharding import PartitionSpec as P

CHANNELS = 4096
RADIX = 64
TAPS = 16
AVG = 32
FRAMES = 8


def dft_table(length):
    index = jnp.arange(length, dtype=jnp.int32)
    phase = index[:, None] * index[None, :] % length
    angle = phase.astype(jnp.float32) * (2.0 * math.pi / length)
    cosine = jnp.cos(angle)
    sine = jnp.sin(angle)
    return jnp.stack([jnp.stack([cosine, sine]), jnp.stack([-sine, cosine])])


def channelize(voltages, fir_taps, first, count):
    width = voltages.shape[1]
    frames = voltages.reshape(2, width, FRAMES + TAPS - 1, CHANNELS)

    def add_tap(tap, filtered):
        window = lax.dynamic_slice_in_dim(frames, first + tap, count, 2).astype(jnp.float32)
        return filtered + fir_taps[tap] * window

    filtered = lax.fori_loop(0, TAPS, add_tap, jnp.zeros((2, width, count, CHANNELS), jnp.float32))
    stacked = filtered.reshape(2, width, count, RADIX, RADIX)
    table = dft_table(RADIX)
    section = jnp.einsum("cwtbn,dcbk->dwtkn", stacked, table, precision=lax.Precision.HIGHEST)
    index = jnp.arange(RADIX, dtype=jnp.int32)
    phase = (index[:, None] * index[None, :]).astype(jnp.float32) * (2.0 * math.pi / CHANNELS)
    tw_cos = jnp.cos(phase)
    tw_sin = jnp.sin(phase)
    turned = jnp.stack(
        [section[0] * tw_cos + section[1] * tw_sin, section[1] * tw_cos - section[0] * tw_sin]
    )
    spectrum = jnp.einsum("cwtkn,dcnm->dwtmk", turned, table, precision=lax.Precision.HIGHEST) * (
        1.0 / RADIX
    )
    return spectrum.astype(jnp.bfloat16).reshape(2, width, count, CHANNELS)


def shards(voltages, fir_taps):
    local = channelize(voltages, fir_taps, 0, FRAMES)
    owned = lax.all_to_all(local, "freq", split_axis=3, concat_axis=1, tiled=True)
    group = owned.shape[3]
    coarse = group // AVG
    scale = 1.0 / (FRAMES * AVG)
    block = owned.shape[1]
    row_count = lax.axis_size("brow")
    col_block = lax.all_gather(owned, "brow", axis=1, tiled=True)
    left_rows = lax.all_gather(owned, "bcol", axis=1, tiled=True)
    left = left_rows.reshape(2, left_rows.shape[1], FRAMES, coarse, AVG)
    right = col_block.reshape(2, col_block.shape[1], FRAMES, coarse, AVG)
    flipped = jnp.stack([-right[1], right[0]])
    real_part = jnp.einsum("cptqa,cutqa->qpu", left, right, preferred_element_type=jnp.float32)
    imag_part = jnp.einsum("cptqa,cutqa->qpu", left, flipped, preferred_element_type=jnp.float32)
    result = jnp.stack([real_part, imag_part]) * scale
    return result.reshape(2, coarse, result.shape[2], row_count, 1, block)


def solution(mesh):
    in_specs = (P(None, ("brow", "bcol", "freq"), None), P())
    out_specs = P(None, "freq", "brow", None, "bcol", None)
    return jax.shard_map(shards, mesh=mesh, in_specs=in_specs, out_specs=out_specs, check_vma=False)
```

profile of v0, /device:TPU:1, one launch (start us, length us, event | category | flops | bytes accessed | tf_op | source)
XLA Modules:
  0.0 201.7 jit_solution(7456410314755574739)
XLA Ops:
  7.0 2.1 %reshape.165 = bf16[2,4,23,4096]{3,2,1,0:T(8,128)(2,1)S(1)} reshape(bf16[2,4,94208]{2,1,0:T(4,128)(2,1)} %param.4) | data formatting | bytes 3014656 | tf_op jit(solution)/shard_map/reshape | solution.py:25
  9.1 23.2 %while.14 = (s32[]{:T(128)}, f32[2,4,8,4096]{3,2,1,0:T(8,128)S(1)}, f32[16,4096]{1,0:T(8,128)}, bf16[2,4,23,4096]{3,2,1,0:T(8,128)(2,1)S(1)}, s32[]{:T(128)}, /*index=5*/s32[]{:T(128)}) while((s32[]{:T(128)}, f32[2,4,8,4096]{3,2,1,0:T(8,128)S(1)}, f32[16,4096]{1,0:T(8,128)}, bf16[2,4,23,4096]{3,2,1,0:T(8,128)(2,1)S(1)}, s32[]{:T(128)}, ...), condition=%wide.region_1.0_spmd.clone, body=%wide.region_0.0_spmd.clone.sunk | while | flops 1048579 | bytes 2670687 | solution.py:31
  9.1 0.9 constant_dynamic-slice_fusion.2
  10.1 0.5 select_add_fusion.2
  10.6 0.9 constant_dynamic-slice_fusion.2
  11.5 0.5 select_add_fusion.2
  12.0 0.9 constant_dynamic-slice_fusion.2
  13.5 0.9 constant_dynamic-slice_fusion.2
  14.9 0.9 constant_dynamic-slice_fusion.2
  15.8 0.5 select_add_fusion.2
  16.4 0.9 constant_dynamic-slice_fusion.2
  17.3 0.5 select_add_fusion.2
  17.8 0.9 constant_dynamic-slice_fusion.2
  18.7 0.5 select_add_fusion.2
  19.3 0.9 constant_dynamic-slice_fusion.2
  20.2 0.5 select_add_fusion.2
  20.7 0.9 constant_dynamic-slice_fusion.2
  21.6 0.5 select_add_fusion.2
  22.2 0.9 constant_dynamic-slice_fusion.2
  23.1 0.5 select_add_fusion.2
  23.6 0.9 constant_dynamic-slice_fusion.2
  24.5 0.5 select_add_fusion.2
  25.1 0.9 constant_dynamic-slice_fusion.2
  26.5 0.9 constant_dynamic-slice_fusion.2
  28.0 0.9 constant_dynamic-slice_fusion.2
  29.4 0.9 constant_dynamic-slice_fusion.2
  30.9 0.9 constant_dynamic-slice_fusion.2
  32.3 0.8 reshape.166
  33.2 2.0 fusion.7
  35.6 3.1 %fusion.12 = bf16[2,4,8,64,64]{4,3,2,1,0:T(8,128)(2,1)S(1)} fusion(f32[1,2,64,64]{2,3,1,0:T(8,128)S(1)} %get-tuple-element.113, f32[1,2,64,64]{2,3,1,0:T(8,128)S(1)} %get-tuple-element.112, f32[1,4,8,64,64]{4,3,2,1,0:T(8,128)S(1)} %get-tuple-element.109, f32[1,4,8,64,64]{4,3,2,1,0:T(8,128)S(1)} %get-tuple-element.108), kind=kOutput, calls=%fused_computation.13 | convolution fusion | flops 403456000 | bytes 1638400 | tf_op jit(solution)/shard_map/cwtkn,dcnm->dwtmk/dot_general | solution.py:42
  38.7 9.3 %copy.45 = bf16[2,4,8,64,64]{2,1,0,4,3:T(4,128)(2,1)} copy(bf16[2,4,8,64,64]{4,3,2,1,0:T(8,128)(2,1)S(1)} %fusion.12) | data formatting | bytes 1048576 | tf_op jit(solution)/shard_map/reshape | solution.py:45
  48.0 10.5 %reshape.177 = bf16[32,2,4096]{2,1,0:T(2,128)(2,1)S(1)} reshape(bf16[4096,2,4,8]{3,2,1,0:T(4,128)(2,1)} %bitcast.66) | data formatting | bytes 1048576
  58.5 27.9 %all_to_all.18 = bf16[32,2,4096]{2,1,0:T(2,128)(2,1)S(1)} all-to-all(bf16[32,2,4096]{2,1,0:T(2,128)(2,1)S(1)} %reshape.177), channel_id=1, replica_groups=mesh['freq'=32,'brow'=2,'bcol'=4] {'freq'}, dimensions={0} | all-to-all | bytes 1048576 | tf_op jit(solution)/shard_map/all_to_all | solution.py:50
  86.4 10.9 %reshape.178 = bf16[4096,2,4,8]{3,2,1,0:T(4,128)(2,1)} reshape(bf16[32,2,4096]{2,1,0:T(2,128)(2,1)S(1)} %all_to_all.18) | data formatting | bytes 1048576
  97.3 10.6 %copy.47 = bf16[2,4,8,32,128]{4,2,1,3,0:T(8,128)(2,1)} copy(bf16[2,4,8,32,128]{2,1,0,4,3:T(4,128)(2,1)} %bitcast.67) | data formatting | bytes 1048576 | tf_op jit(solution)/shard_map/all_to_all | solution.py:50
  108.1 0.5 all-gather.3.cloned.1.call-update
  108.7 25.4 %all-gather.5.cloned.1.call-done = bf16[2,256,8,128]{3,2,1,0:T(8,128)(2,1)} async-done(((bf16[2,128,8,128]{3,2,1,0:T(8,128)(2,1)}), bf16[2,256,8,128]{3,2,1,0:T(8,128)(2,1)}) %all-gather.5.cloned.1.call-update) | async-done | bytes 1048592 | tf_op jit(solution)/shard_map/all_gather | solution.py:56
  134.1 1.4 slice_negate_fusion
  135.5 1.1 copy.36
  136.6 1.1 copy.37
  137.7 0.7 copy.35
  138.4 29.0 %all-gather.3.cloned.1.call-done = bf16[2,512,8,128]{3,2,1,0:T(8,128)(2,1)} async-done(((bf16[2,128,8,128]{3,2,1,0:T(8,128)(2,1)}), bf16[2,512,8,128]{3,2,1,0:T(8,128)(2,1)}) %all-gather.3.cloned.1.call-update) | async-done | bytes 2097168 | tf_op jit(solution)/shard_map/all_gather | solution.py:57
  167.4 3.0 %copy.34 = bf16[2,512,8,128]{1,3,2,0:T(8,128)(2,1)S(1)} copy(bf16[2,512,8,128]{3,2,1,0:T(8,128)(2,1)} %all-gather.3.cloned.1.call-done) | data formatting | bytes 4194304 | tf_op jit(solution)/shard_map/all_gather | solution.py:57
  170.4 2.1 %fusion.33 = f32[4,512,256,1,1]{1,2,0,4,3:T(8,128)} fusion(bf16[2,512,8,4,32]{1,4,3,2,0:T(8,128)(2,1)S(1)} %bitcast.68, bf16[2,256,8,4,32]{1,4,3,2,0:T(8,128)(2,1)S(1)} %bitcast.74), kind=kOutput, calls=%fused_computation.42 | convolution fusion | flops 536870912 | bytes 5242880 | tf_op jit(solution)/shard_map/cptqa,cutqa->qpu/dot_general | solution.py:61
  172.5 6.1 %copy.38 = f32[1,4,512,2,1,128]{5,4,3,2,1,0:T(1,128)} copy(f32[1,4,512,2,1,128]{2,5,3,1,4,0:T(8,128)} %bitcast.71) | data formatting | bytes 4194304 | tf_op jit(solution)/shard_map/stack | solution.py:63
  178.7 2.1 %fusion.15 = f32[4,512,256,1,1]{1,2,0,4,3:T(8,128)} fusion(bf16[2,512,8,4,32]{1,4,3,2,0:T(8,128)(2,1)S(1)} %bitcast.69, bf16[1,256,8,4,32]{1,4,3,2,0:T(8,128)(2,1)S(1)} %bitcast.76, bf16[1,256,8,4,32]{1,4,3,2,0:T(8,128)(2,1)S(1)} %bitcast.75), kind=kOutput, calls=%fused_computation.14 | convolution fusion | flops 537395200 | bytes 5242880 | tf_op jit(solution)/shard_map/cptqa,cutqa->qpu/dot_general | solution.py:62
  180.7 6.2 %copy.39 = f32[1,4,512,2,1,128]{5,4,3,2,1,0:T(1,128)} copy(f32[1,4,512,2,1,128]{2,5,3,1,4,0:T(8,128)} %bitcast.70) | data formatting | bytes 4194304 | tf_op jit(solution)/shard_map/stack | solution.py:63
  186.9 7.9 %maximum_multiply_fusion = f32[2,4,512,2,1,128]{5,4,3,2,1,0:T(1,128)} fusion(f32[1,4,512,2,1,128]{5,4,3,2,1,0:T(1,128)} %copy.39, f32[1,4,512,2,1,128]{5,4,3,2,1,0:T(1,128)S(1)} %copy-done), kind=kLoop, calls=%fused_computation.2 | loop fusion | flops 2097152 | bytes 8388608 | tf_op jit(solution)/shard_map/mul | solution.py:63
  (24 shorter events, 4.6 us)
Async XLA Ops:
  6.5 127.5 %all-gather.5.cloned.1.call-start = ((), (), s32[]{:S(2)}) async-start(), calls=%async_computation.2 | async-start | bytes 1572864 | tf_op jit(solution)/shard_map/all_gather | solution.py:56
  107.9 59.5 %all-gather.3.cloned.1.call-start = ((), (), s32[]{:S(2)}) async-start(), calls=%async_computation.1 | async-start | bytes 2621440 | tf_op jit(solution)/shard_map/all_gather | solution.py:57
  134.1 3.7 %copy-start.1 = (bf16[2,256,8,128]{3,2,1,0:T(8,128)(2,1)S(1)}, bf16[2,256,8,128]{3,2,1,0:T(8,128)(2,1)}, u32[]{:S(2)}) copy-start(bf16[2,256,8,128]{3,2,1,0:T(8,128)(2,1)} %all-gather.5.cloned.1.call-done) | copy-start | bytes 3145732
  172.5 6.2 %copy-start.2 = (bf16[1,256,8,128]{1,3,2,0:T(8,128)(2,1)S(1)}, bf16[1,256,8,128]{1,3,2,0:T(8,128)(2,1)}, u32[]{:S(2)}) copy-start(bf16[1,256,8,128]{1,3,2,0:T(8,128)(2,1)} %copy.36) | copy-start | bytes 1572868
  172.5 6.2 %copy-start.3 = (bf16[1,256,8,128]{1,3,2,0:T(8,128)(2,1)S(1)}, bf16[1,256,8,128]{1,3,2,0:T(8,128)(2,1)}, u32[]{:S(2)}) copy-start(bf16[1,256,8,128]{1,3,2,0:T(8,128)(2,1)} %copy.37) | copy-start | bytes 1572868
  180.7 6.2 %copy-start = (f32[1,4,512,2,1,128]{5,4,3,2,1,0:T(1,128)S(1)}, f32[1,4,512,2,1,128]{5,4,3,2,1,0:T(1,128)}, u32[]{:S(2)}) copy-start(f32[1,4,512,2,1,128]{5,4,3,2,1,0:T(1,128)} %copy.38) | copy-start | bytes 6291460
Sparse Core Ops, SparseCore 0:
  108.0 25.9 all-gather.4
  135.9 31.4 all-gather.2
where the time goes:
time: 203 us; the launch traced here: 202 us
  local copies, waits for them, and re-layouts  77.2 us (38%)
  waiting for transfers between devices  55 us (27%)
  blocking collectives  27.9 us (14%)
  other arithmetic  18.2 us (9%)
  between operations  13.5 us (7%)
  matrix products  9.25 us (5%)
    all_gather x1, waiting for transfers between devices, shards(): left_rows = lax.all_gather(owned, 'bcol', axis=1, tiled=True)  29 us
    all_to_all x1, blocking collectives, shards(): lax.all_to_all(local, 'freq', split_axis=3, concat_axis=1, tiled=True)  27.9 us
    all_gather x1, waiting for transfers between devices, shards(): col_block = lax.all_gather(owned, 'brow', axis=1, tiled=True)  25.4 us
    unnamed x10, local copies, waits for them, and re-layouts  21.4 us
    dynamic_slice x16, local copies, waits for them, and re-layouts, add_tap(): return filtered + fir_taps[tap] * window  14.8 us
    another operation x2, local copies, waits for them, and re-layouts, shards(): result = jnp.stack([real_part, imag_part]) * scale  12.3 us
    all_to_all x1, local copies, waits for them, and re-layouts, shards(): lax.all_to_all(local, 'freq', split_axis=3, concat_axis=1, tiled=True)  10.6 us
    reshape x1, local copies, waits for them, and re-layouts, channelize(): return spectrum.astype(jnp.bfloat16).reshape(2, width, count, CHANNELS)  9.33 us
  transfers between devices with their start and end apart: 2, of which 2 were waited for; matrix products, arithmetic and copies ran while one was open for 2% of the time, Pallas kernels for 0%

commit v1 on v0

--- a/solution.py
+++ b/solution.py
@@ -3,6 +3,7 @@
 import jax.numpy as jnp
 from jax import lax
 from jax.sharding import PartitionSpec as P
+from jax.lax import all_to_all, psum
 
 CHANNELS = 4096
 RADIX = 64
@@ -47,7 +48,12 @@
 
 def shards(voltages, fir_taps):
     local = channelize(voltages, fir_taps, 0, FRAMES)
-    owned = lax.all_to_all(local, "freq", split_axis=3, concat_axis=1, tiled=True)
+    owned = jnp.concatenate(
+        all_to_all(
+            jnp.stack(jnp.split(local, psum(1, "freq"), 3)), "freq", concat_axis=0, split_axis=0
+        ),
+        1,
+    )
     group = owned.shape[3]
     coarse = group // AVG
     scale = 1.0 / (FRAMES * AVG)

time: 203 us -> 163 us (0.80)
  local copies, waits for them, and re-layouts: 77.2 us -> 38 us
    unnamed x10 -> x39, local copies, waits for them, and re-layouts: 21.4 us -> 0.43 us
    all_to_all x1, local copies, waits for them, and re-layouts: 10.6 us -> 0.83 us  [shards(): all_to_all(jnp.stack(jnp.split(local, psum(1, 'freq'), 3)), 'freq', conca...]
    reshape x1, local copies, waits for them, and re-layouts: 9.33 us -> 0.81 us  [channelize(): return spectrum.astype(jnp.bfloat16).reshape(2, width, count, CHANNELS)]
  transfers between devices with their start and end apart: 2 -> 2, of which waited for: 2 -> 2; matrix products, arithmetic and copies ran while one was open for 2% -> 3% of each run, Pallas kernels for 0% -> 0%
where the time goes in v1:
time: 163 us
  waiting for transfers between devices  55 us (34%)
  local copies, waits for them, and re-layouts  38 us (23%)
  blocking collectives  27.9 us (17%)
  other arithmetic  18.2 us (11%)
  between operations  13.7 us (8%)
  matrix products  9.25 us (6%)
    all_gather x1, waiting for transfers between devices, shards(): left_rows = lax.all_gather(owned, 'bcol', axis=1, tiled=True)  29 us
    all_to_all x1, blocking collectives, shards(): all_to_all(jnp.stack(jnp.split(local, psum(1, 'freq'), 3)), 'freq', conca...  27.9 us
    all_gather x1, waiting for transfers between devices, shards(): col_block = lax.all_gather(owned, 'brow', axis=1, tiled=True)  25.4 us
    dynamic_slice x16, local copies, waits for them, and re-layouts, add_tap(): return filtered + fir_taps[tap] * window  14.8 us
    another operation x2, local copies, waits for them, and re-layouts, shards(): result = jnp.stack([real_part, imag_part]) * scale  12.3 us
    add x16, other arithmetic, add_tap(): return filtered + fir_taps[tap] * window  8.05 us
    mul x1, other arithmetic, shards(): result = jnp.stack([real_part, imag_part]) * scale  7.92 us
  transfers between devices with their start and end apart: 2, of which 2 were waited for; matrix products, arithmetic and copies ran while one was open for 3% of the time, Pallas kernels for 0%

profile of v1, /device:TPU:1, one launch (start us, length us, event | category | flops | bytes accessed | tf_op | source)
XLA Modules:
  0.0 162.6 jit_solution(13767817322749985334)
XLA Ops:
  7.0 2.1 %reshape.171 = bf16[2,4,23,4096]{3,2,1,0:T(8,128)(2,1)S(1)} reshape(bf16[2,4,94208]{2,1,0:T(4,128)(2,1)} %param.4) | data formatting | bytes 3014656 | tf_op jit(solution)/shard_map/reshape | solution.py:26
  9.1 23.2 %while.14 = (s32[]{:T(128)}, f32[2,4,8,4096]{3,2,1,0:T(8,128)S(1)}, f32[16,4096]{1,0:T(8,128)}, bf16[2,4,23,4096]{3,2,1,0:T(8,128)(2,1)S(1)}, s32[]{:T(128)}, /*index=5*/s32[]{:T(128)}) while((s32[]{:T(128)}, f32[2,4,8,4096]{3,2,1,0:T(8,128)S(1)}, f32[16,4096]{1,0:T(8,128)}, bf16[2,4,23,4096]{3,2,1,0:T(8,128)(2,1)S(1)}, s32[]{:T(128)}, ...), condition=%wide.region_1.0_spmd.clone, body=%wide.region_0.0_spmd.clone.sunk | while | flops 1048579 | bytes 2670687 | solution.py:32
  9.1 0.9 constant_dynamic-slice_fusion.2
  10.1 0.5 select_add_fusion.2
  10.6 0.9 constant_dynamic-slice_fusion.2
  11.5 0.5 select_add_fusion.2
  12.0 0.9 constant_dynamic-slice_fusion.2
  13.5 0.9 constant_dynamic-slice_fusion.2
  14.9 0.9 constant_dynamic-slice_fusion.2
  15.8 0.5 select_add_fusion.2
  16.4 0.9 constant_dynamic-slice_fusion.2
  17.3 0.5 select_add_fusion.2
  17.8 0.9 constant_dynamic-slice_fusion.2
  18.7 0.5 select_add_fusion.2
  19.3 0.9 constant_dynamic-slice_fusion.2
  20.2 0.5 select_add_fusion.2
  20.7 0.9 constant_dynamic-slice_fusion.2
  21.6 0.5 select_add_fusion.2
  22.2 0.9 constant_dynamic-slice_fusion.2
  23.1 0.5 select_add_fusion.2
  23.6 0.9 constant_dynamic-slice_fusion.2
  24.5 0.5 select_add_fusion.2
  25.1 0.9 constant_dynamic-slice_fusion.2
  26.0 0.5 select_add_fusion.2
  26.5 0.9 constant_dynamic-slice_fusion.2
  27.4 0.5 select_add_fusion.2
  28.0 0.9 constant_dynamic-slice_fusion.2
  29.4 0.9 constant_dynamic-slice_fusion.2
  30.9 0.9 constant_dynamic-slice_fusion.2
  32.3 0.8 reshape.172
  33.2 2.0 %fusion.7 = f32[2,4,8,64,64]{4,3,2,1,0:T(8,128)S(1)} fusion(f32[2,4,8,64,64]{4,3,2,1,0:T(8,128)S(1)} %reshape.172, f32[1,2,64,64]{2,3,1,0:T(8,128)S(1)} %get-tuple-element.113, f32[1,2,64,64]{2,3,1,0:T(8,128)S(1)} %get-tuple-element.112), kind=kOutput, calls=%fused_computation.12 | convolution fusion | flops 402669568 | bytes 2162688 | tf_op jit(solution)/shard_map/cwtbn,dcbk->dwtkn/dot_general | solution.py:35
  35.6 3.1 %fusion.12 = bf16[2,4,8,64,64]{4,3,2,1,0:T(8,128)(2,1)S(1)} fusion(f32[1,2,64,64]{2,3,1,0:T(8,128)S(1)} %get-tuple-element.113, f32[1,2,64,64]{2,3,1,0:T(8,128)S(1)} %get-tuple-element.112, f32[1,4,8,64,64]{4,3,2,1,0:T(8,128)S(1)} %get-tuple-element.109, f32[1,4,8,64,64]{4,3,2,1,0:T(8,128)S(1)} %get-tuple-element.108), kind=kOutput, calls=%fused_computation.13 | convolution fusion | flops 403456000 | bytes 1638400 | tf_op jit(solution)/shard_map/cwtkn,dcnm->dwtmk/dot_general | solution.py:43
  38.7 0.8 reshape.173
  40.1 27.9 %all_to_all.5 = bf16[32,2,4,8,128]{4,3,2,1,0:T(8,128)(2,1)S(1)} all-to-all(bf16[32,2,4,8,128]{4,3,2,1,0:T(8,128)(2,1)S(1)} %constant_dynamic-update-slice_fusion), channel_id=1, replica_groups=mesh['freq'=32,'brow'=2,'bcol'=4] {'freq'}, dimensions={0} | all-to-all | bytes 1048576 | tf_op jit(solution)/shard_map/all_to_all | solution.py:52
  68.0 0.8 copy.53
  69.1 0.5 all-gather.3.cloned.1.call-update
  69.6 25.4 %all-gather.5.cloned.1.call-done = bf16[2,256,8,128]{3,2,1,0:T(8,128)(2,1)} async-done(((bf16[2,128,8,128]{3,2,1,0:T(8,128)(2,1)}), bf16[2,256,8,128]{3,2,1,0:T(8,128)(2,1)}) %all-gather.5.cloned.1.call-update) | async-done | bytes 1048592 | tf_op jit(solution)/shard_map/all_gather | solution.py:62
  95.0 1.4 slice_negate_fusion
  96.4 1.1 copy.56
  97.6 1.1 copy.57
  98.7 0.7 copy.55
  99.4 29.0 %all-gather.3.cloned.1.call-done = bf16[2,512,8,128]{3,2,1,0:T(8,128)(2,1)} async-done(((bf16[2,128,8,128]{3,2,1,0:T(8,128)(2,1)}), bf16[2,512,8,128]{3,2,1,0:T(8,128)(2,1)}) %all-gather.3.cloned.1.call-update) | async-done | bytes 2097168 | tf_op jit(solution)/shard_map/all_gather | solution.py:63
  128.4 3.0 %copy.54 = bf16[2,512,8,128]{1,3,2,0:T(8,128)(2,1)S(1)} copy(bf16[2,512,8,128]{3,2,1,0:T(8,128)(2,1)} %all-gather.3.cloned.1.call-done) | data formatting | bytes 4194304 | tf_op jit(solution)/shard_map/all_gather | solution.py:63
  131.4 2.1 %fusion.33 = f32[4,512,256,1,1]{1,2,0,4,3:T(8,128)} fusion(bf16[2,512,8,4,32]{1,4,3,2,0:T(8,128)(2,1)S(1)} %bitcast.191, bf16[2,256,8,4,32]{1,4,3,2,0:T(8,128)(2,1)S(1)} %bitcast.197), kind=kOutput, calls=%fused_computation.106 | convolution fusion | flops 536870912 | bytes 5242880 | tf_op jit(solution)/shard_map/cptqa,cutqa->qpu/dot_general | solution.py:67
  133.5 6.1 %copy.58 = f32[1,4,512,2,1,128]{5,4,3,2,1,0:T(1,128)} copy(f32[1,4,512,2,1,128]{2,5,3,1,4,0:T(8,128)} %bitcast.194) | data formatting | bytes 4194304 | tf_op jit(solution)/shard_map/stack | solution.py:69
  139.6 2.1 %fusion.15 = f32[4,512,256,1,1]{1,2,0,4,3:T(8,128)} fusion(bf16[2,512,8,4,32]{1,4,3,2,0:T(8,128)(2,1)S(1)} %bitcast.192, bf16[1,256,8,4,32]{1,4,3,2,0:T(8,128)(2,1)S(1)} %bitcast.199, bf16[1,256,8,4,32]{1,4,3,2,0:T(8,128)(2,1)S(1)} %bitcast.198), kind=kOutput, calls=%fused_computation.14 | convolution fusion | flops 537395200 | bytes 5242880 | tf_op jit(solution)/shard_map/cptqa,cutqa->qpu/dot_general | solution.py:68
  141.7 6.2 %copy.59 = f32[1,4,512,2,1,128]{5,4,3,2,1,0:T(1,128)} copy(f32[1,4,512,2,1,128]{2,5,3,1,4,0:T(8,128)} %bitcast.193) | data formatting | bytes 4194304 | tf_op jit(solution)/shard_map/stack | solution.py:69
  147.9 7.9 %maximum_multiply_fusion = f32[2,4,512,2,1,128]{5,4,3,2,1,0:T(1,128)} fusion(f32[1,4,512,2,1,128]{5,4,3,2,1,0:T(1,128)} %copy.59, f32[1,4,512,2,1,128]{5,4,3,2,1,0:T(1,128)S(1)} %copy-done), kind=kLoop, calls=%fused_computation.2 | loop fusion | flops 2097152 | bytes 8388608 | tf_op jit(solution)/shard_map/mul | solution.py:69
  (54 shorter events, 4.1 us)
Async XLA Ops:
  6.5 88.5 %all-gather.5.cloned.1.call-start = ((), (), s32[]{:S(2)}) async-start(), calls=%async_computation.2 | async-start | bytes 1572864 | tf_op jit(solution)/shard_map/all_gather | solution.py:62
  68.9 59.5 %all-gather.3.cloned.1.call-start = ((), (), s32[]{:S(2)}) async-start(), calls=%async_computation.1 | async-start | bytes 2621440 | tf_op jit(solution)/shard_map/all_gather | solution.py:63
  95.0 3.7 %copy-start.1 = (bf16[2,256,8,128]{3,2,1,0:T(8,128)(2,1)S(1)}, bf16[2,256,8,128]{3,2,1,0:T(8,128)(2,1)}, u32[]{:S(2)}) copy-start(bf16[2,256,8,128]{3,2,1,0:T(8,128)(2,1)} %all-gather.5.cloned.1.call-done) | copy-start | bytes 3145732
  133.5 6.2 %copy-start.2 = (bf16[1,256,8,128]{1,3,2,0:T(8,128)(2,1)S(1)}, bf16[1,256,8,128]{1,3,2,0:T(8,128)(2,1)}, u32[]{:S(2)}) copy-start(bf16[1,256,8,128]{1,3,2,0:T(8,128)(2,1)} %copy.56) | copy-start | bytes 1572868
  133.5 6.2 %copy-start.3 = (bf16[1,256,8,128]{1,3,2,0:T(8,128)(2,1)S(1)}, bf16[1,256,8,128]{1,3,2,0:T(8,128)(2,1)}, u32[]{:S(2)}) copy-start(bf16[1,256,8,128]{1,3,2,0:T(8,128)(2,1)} %copy.57) | copy-start | bytes 1572868
  141.7 6.2 %copy-start = (f32[1,4,512,2,1,128]{5,4,3,2,1,0:T(1,128)S(1)}, f32[1,4,512,2,1,128]{5,4,3,2,1,0:T(1,128)}, u32[]{:S(2)}) copy-start(f32[1,4,512,2,1,128]{5,4,3,2,1,0:T(1,128)} %copy.58) | copy-start | bytes 6291460
Sparse Core Ops, SparseCore 0:
  69.0 25.9 all-gather.4
  96.8 31.4 all-gather.2
